TPU v7x, 128 devices: a whole 4x4x4 slice. The times are simulated.
128 devices in a mesh: seq: 32 (over x, y, core), trk: 4 (over z).
Axes of the slice: x: 4, y: 4, z: 4, core: 2. Of those that a mesh axis runs over, the one named last changes fastest.
Arguments:
- trunk_input: bfloat16 [12288, 1536], P('seq', 'trk'), may hold values from -6 to 6
- conv_in: bfloat16 [6, 3, 768, 1536], P(None, None, 'trk'), may hold values from -0.09375 to 0.09375
- conv_bias: bfloat16 [6, 768], P(None, 'trk'), may hold values from -3 to 3
- conv_out: bfloat16 [6, 768, 1536], P(None, 'trk'), may hold values from -0.21875 to 0.21875
- projection_bias: bfloat16 [6, 1536], P(None, 'trk'), may hold values from -3 to 3
- head_weight: bfloat16 [1536, 4096], P(None, 'trk'), may hold values from -0.15625 to 0.15625
- head_bias: bfloat16 [4096], P('trk'), may hold values from -4 to 4
- exon_bins: int32 [256, 64], P('seq'), may hold values from -1 to 12287, as said below
Outputs:
- coverage: bfloat16 [12288, 4096], P('seq', 'trk')
- gene_cov: float32 [256, 4096], P('seq', 'trk')
Inputs may be any that keep to these rules, and one draw needn't show every extreme that they name: `exon_bins`: row g lists gene g's exon bins in increasing order, then -1 in the unused entries; every gene has at least one exon bin and some gene has exactly 64. The genes of rows 8 * o to 8 * (o + 1) - 1 are owned by index o of seq.
All inputs are finite; a program needn't handle non-finite values.
Results may differ from a plain program's by a relative error of at most 0.024.
Values may be sent and summed in bfloat16 or wider, within the bound.
A program may use at most 128 MiB of HBM per device.

v0:
```python
import jax
import jax.numpy as jnp
from jax import lax
from jax.sharding import PartitionSpec as P

RESIDUAL_BLOCKS = 6
BASE_DILATION = 2


def extended(cells, sides, width):
    for axis, dim in sides:
        count = lax.axis_size(axis)
        ends = count - 1
        head = lax.slice_in_dim(cells, 0, width, axis=dim)
        tail = lax.slice_in_dim(cells, cells.shape[dim] - width, cells.shape[dim], axis=dim)
        cells = jnp.concatenate(
            [
                lax.ppermute(tail, axis, [(i, (i + 1) % count) for i in range(ends)]),
                cells,
                lax.ppermute(head, axis, [((i + 1) % count, i) for i in range(ends)]),
            ],
            axis=dim,
        )
    return cells


def contract_last(rows, kernel):
    return lax.dot_general(
        rows, kernel, (((1,), (1,)), ((), ())), preferred_element_type=jnp.float32
    )


def dilated_inner(trunk, conv_in, block_layer_index, dilation_step):
    bin_rows = trunk.shape[0]
    gathered = lax.all_gather(trunk, "trk", axis=1, tiled=True)
    padded = extended(gathered, (("seq", 0),), dilation_step)
    inner = jnp.zeros((bin_rows, conv_in.shape[2]), jnp.float32)
    for tap_index in range(3):
        window = padded[tap_index * dilation_step : tap_index * dilation_step + bin_rows]
        inner = inner + contract_last(window, conv_in[block_layer_index, tap_index])
    return inner


def exon_onehot(gene_block, width_now):
    exon_matches = gene_block[:, :, None] == jnp.arange(width_now, dtype=jnp.int32)[None, None, :]
    return jnp.sum(exon_matches.astype(jnp.float32), axis=1).astype(jnp.bfloat16)


def shards(
    trunk_input, conv_in, conv_bias, conv_out, projection_bias, head_weight, head_bias, exon_bins
):
    trunk = trunk_input
    for block_layer_index in range(RESIDUAL_BLOCKS):
        dilation_step = BASE_DILATION * 2**block_layer_index
        inner = dilated_inner(trunk, conv_in, block_layer_index, dilation_step)
        activation = jax.nn.gelu(
            inner + conv_bias[block_layer_index].astype(jnp.float32), approximate=True
        ).astype(jnp.bfloat16)
        partial_value = jnp.dot(
            activation, conv_out[block_layer_index], preferred_element_type=jnp.float32
        )
        summed = lax.psum_scatter(
            partial_value.astype(jnp.bfloat16), "trk", scatter_dimension=1, tiled=True
        ).astype(jnp.float32)
        trunk = (
            trunk.astype(jnp.float32)
            + summed
            + projection_bias[block_layer_index].astype(jnp.float32)
        ).astype(jnp.bfloat16)
    logits = jnp.dot(
        lax.all_gather(trunk, "trk", axis=1, tiled=True),
        head_weight,
        preferred_element_type=jnp.float32,
    )
    coverage = jax.nn.softplus(logits + head_bias.astype(jnp.float32)).astype(jnp.bfloat16)
    shard_rows = lax.all_gather(coverage, "seq", axis=0, tiled=True)
    onehot = exon_onehot(exon_bins, shard_rows.shape[0])
    gene_sum = jnp.dot(onehot, shard_rows, preferred_element_type=jnp.float32)
    counts = jnp.sum((exon_bins >= 0).astype(jnp.float32), axis=1)
    gene_cov = gene_sum / counts[:, None]
    return (coverage, gene_cov)


def solution(mesh):
    in_specs = (
        P("seq", "trk"),
        P(None, None, "trk", None),
        P(None, "trk"),
        P(None, "trk", None),
        P(None, "trk"),
        P(None, "trk"),
        P("trk"),
        P("seq", None),
    )
    out_specs = (P("seq", "trk"), P("seq", "trk"))
    return jax.shard_map(shards, mesh=mesh, in_specs=in_specs, out_specs=out_specs, check_vma=False)
```

profile of v0, /device:TPU:1, one launch (start us, length us, event | category | flops | bytes accessed | tf_op | source)
XLA Modules:
  0.0 589.5 jit_solution(15093628703576068689)
XLA Ops:
  8.9 26.9 %all-gather.9.cloned.1.call-done = bf16[384,1536]{1,0:T(8,128)(2,1)} async-done(((bf16[384,384]{1,0:T(8,128)(2,1)}), bf16[384,1536]{1,0:T(8,128)(2,1)}) %all-gather.9.cloned.1.call-update) | async-done | bytes 1179664 | tf_op jit(solution)/shard_map/all_gather | solution.py:35
  36.6 6.0 %collective-permute-start = (bf16[2,1536]{1,0:T(2,128)(2,1)S(1)}, bf16[2,1536]{1,0:T(2,128)(2,1)S(1)}, u32[]{:S(2)}, u32[]{:S(2)}) collective-permute-start(bf16[2,1536]{1,0:T(2,128)(2,1)S(1)} %get-tuple-element.18), channel_id=1, source_target_pairs={{0,4},{4,8},{8,12},{12,16},{16,20},{20,24},{24,28},{28,32},{32,36}... | collective-permute-start | bytes 18440 | tf_op jit(solution)/shard_map/ppermute | solution.py:18
  49.9 3.9 convolution_convert_fusion.5
  56.9 23.2 %reduce-scatter.19.cloned.1.call-done = bf16[384,384]{1,0:T(8,128)(2,1)} async-done(((bf16[1536,384]{1,0:T(8,128)(2,1)}), bf16[384,384]{1,0:T(8,128)(2,1)}) %reduce-scatter.19.cloned.1.call-update) | async-done | bytes 294928
  83.8 24.2 %all-gather.11.cloned.1.call-done = bf16[384,1536]{1,0:T(8,128)(2,1)} async-done(((bf16[384,384]{1,0:T(8,128)(2,1)}), bf16[384,1536]{1,0:T(8,128)(2,1)}) %all-gather.11.cloned.1.call-update) | async-done | bytes 1179664 | tf_op jit(solution)/shard_map/all_gather | solution.py:35
  108.9 6.0 %collective-permute-start.2 = (bf16[4,1536]{1,0:T(4,128)(2,1)S(1)}, bf16[4,1536]{1,0:T(4,128)(2,1)S(1)}, u32[]{:S(2)}, u32[]{:S(2)}) collective-permute-start(bf16[4,1536]{1,0:T(4,128)(2,1)S(1)} %get-tuple-element.16), channel_id=1, source_target_pairs={{0,4},{4,8},{8,12},{12,16},{16,20},{20,24},{24,28},{28,32},{32,36}... | collective-permute-start | bytes 36872 | tf_op jit(solution)/shard_map/ppermute | solution.py:18
  116.8 2.7 fusion.65
  122.2 4.0 convolution_convert_fusion.4
  128.7 23.4 %reduce-scatter.21.cloned.1.call-done = bf16[384,384]{1,0:T(8,128)(2,1)} async-done(((bf16[1536,384]{1,0:T(8,128)(2,1)}), bf16[384,384]{1,0:T(8,128)(2,1)}) %reduce-scatter.21.cloned.1.call-update) | async-done | bytes 294928
  155.8 24.6 %all-gather.13.cloned.1.call-done = bf16[384,1536]{1,0:T(8,128)(2,1)} async-done(((bf16[384,384]{1,0:T(8,128)(2,1)}), bf16[384,1536]{1,0:T(8,128)(2,1)}) %all-gather.13.cloned.1.call-update) | async-done | bytes 1179664 | tf_op jit(solution)/shard_map/all_gather | solution.py:35
  181.2 6.0 %collective-permute-start.4 = (bf16[8,1536]{1,0:T(8,128)(2,1)S(1)}, bf16[8,1536]{1,0:T(8,128)(2,1)S(1)}, u32[]{:S(2)}, u32[]{:S(2)}) collective-permute-start(bf16[8,1536]{1,0:T(8,128)(2,1)S(1)} %get-tuple-element.14), channel_id=1, source_target_pairs={{0,4},{4,8},{8,12},{12,16},{16,20},{20,24},{24,28},{28,32},{32,36}... | collective-permute-start | bytes 73736 | tf_op jit(solution)/shard_map/ppermute | solution.py:18
  189.2 2.7 fusion.60
  194.7 4.0 convolution_convert_fusion.3
  201.1 23.8 %reduce-scatter.23.cloned.1.call-done = bf16[384,384]{1,0:T(8,128)(2,1)} async-done(((bf16[1536,384]{1,0:T(8,128)(2,1)}), bf16[384,384]{1,0:T(8,128)(2,1)}) %reduce-scatter.23.cloned.1.call-update) | async-done | bytes 294928
  228.6 24.2 %all-gather.15.cloned.1.call-done = bf16[384,1536]{1,0:T(8,128)(2,1)} async-done(((bf16[384,384]{1,0:T(8,128)(2,1)}), bf16[384,1536]{1,0:T(8,128)(2,1)}) %all-gather.15.cloned.1.call-update) | async-done | bytes 1179664 | tf_op jit(solution)/shard_map/all_gather | solution.py:35
  253.7 6.0 %collective-permute-start.6 = (bf16[16,1536]{1,0:T(8,128)(2,1)S(1)}, bf16[16,1536]{1,0:T(8,128)(2,1)S(1)}, u32[]{:S(2)}, u32[]{:S(2)}) collective-permute-start(bf16[16,1536]{1,0:T(8,128)(2,1)S(1)} %get-tuple-element.12), channel_id=1, source_target_pairs={{0,4},{4,8},{8,12},{12,16},{16,20},{20,24},{24,28},{28,32},{32,36}... | collective-permute-start | bytes 147464 | tf_op jit(solution)/shard_map/ppermute | solution.py:18
  261.6 2.7 fusion.55
  267.5 3.9 convolution_convert_fusion.2
  273.9 23.8 %reduce-scatter.25.cloned.1.call-done = bf16[384,384]{1,0:T(8,128)(2,1)} async-done(((bf16[1536,384]{1,0:T(8,128)(2,1)}), bf16[384,384]{1,0:T(8,128)(2,1)}) %reduce-scatter.25.cloned.1.call-update) | async-done | bytes 294928
  301.3 24.2 %all-gather.17.cloned.1.call-done = bf16[384,1536]{1,0:T(8,128)(2,1)} async-done(((bf16[384,384]{1,0:T(8,128)(2,1)}), bf16[384,1536]{1,0:T(8,128)(2,1)}) %all-gather.17.cloned.1.call-update) | async-done | bytes 1179664 | tf_op jit(solution)/shard_map/all_gather | solution.py:35
  326.5 6.1 %collective-permute-start.8 = (bf16[32,1536]{1,0:T(8,128)(2,1)S(1)}, bf16[32,1536]{1,0:T(8,128)(2,1)S(1)}, u32[]{:S(2)}, u32[]{:S(2)}) collective-permute-start(bf16[32,1536]{1,0:T(8,128)(2,1)S(1)} %get-tuple-element.10), channel_id=1, source_target_pairs={{0,4},{4,8},{8,12},{12,16},{16,20},{20,24},{24,28},{28,32},{32,36}... | collective-permute-start | bytes 294920 | tf_op jit(solution)/shard_map/ppermute | solution.py:18
  340.9 3.9 convolution_convert_fusion.1
  347.3 23.6 %reduce-scatter.27.cloned.1.call-done = bf16[384,384]{1,0:T(8,128)(2,1)} async-done(((bf16[1536,384]{1,0:T(8,128)(2,1)}), bf16[384,384]{1,0:T(8,128)(2,1)}) %reduce-scatter.27.cloned.1.call-update) | async-done | bytes 294928
  374.6 24.4 %all-gather.19.cloned.1.call-done = bf16[384,1536]{1,0:T(8,128)(2,1)} async-done(((bf16[384,384]{1,0:T(8,128)(2,1)}), bf16[384,1536]{1,0:T(8,128)(2,1)}) %all-gather.19.cloned.1.call-update) | async-done | bytes 1179664 | tf_op jit(solution)/shard_map/all_gather | solution.py:35
  400.1 6.1 %collective-permute-start.10 = (bf16[64,1536]{1,0:T(8,128)(2,1)S(1)}, bf16[64,1536]{1,0:T(8,128)(2,1)S(1)}, u32[]{:S(2)}, u32[]{:S(2)}) collective-permute-start(bf16[64,1536]{1,0:T(8,128)(2,1)S(1)} %get-tuple-element.8), channel_id=1, source_target_pairs={{0,4},{4,8},{8,12},{12,16},{16,20},{20,24},{24,28},{28,32},{32,36}... | collective-permute-start | bytes 589832 | tf_op jit(solution)/shard_map/ppermute | solution.py:18
  415.5 3.9 convolution_convert_fusion
  421.9 23.4 %reduce-scatter.29.cloned.1.call-done = bf16[384,384]{1,0:T(8,128)(2,1)} async-done(((bf16[1536,384]{1,0:T(8,128)(2,1)}), bf16[384,384]{1,0:T(8,128)(2,1)}) %reduce-scatter.29.cloned.1.call-update) | async-done | bytes 294928
  449.0 24.6 %all-gather.21.cloned.1.call-done = bf16[384,1536]{1,0:T(8,128)(2,1)} async-done(((bf16[384,384]{1,0:T(8,128)(2,1)}), bf16[384,1536]{1,0:T(8,128)(2,1)}) %all-gather.21.cloned.1.call-update) | async-done | bytes 1179664 | tf_op jit(solution)/shard_map/all_gather | solution.py:71
  473.6 4.2 fusion
  478.0 4.9 convert_reduce_fusion
  482.9 89.5 %all-gather.23.cloned.1.call-done = bf16[12288,1024]{1,0:T(8,128)(2,1)} async-done(((bf16[384,1024]{1,0:T(8,128)(2,1)}), bf16[12288,1024]{1,0:T(8,128)(2,1)}) %all-gather.23.cloned.1.call-update) | async-done | bytes 25165840 | tf_op jit(solution)/shard_map/all_gather | solution.py:76
  572.4 10.5 %convolution_divide_fusion = f32[8,1024]{1,0:T(8,128)} fusion(bf16[12288,1024]{1,0:T(8,128)(2,1)} %all-gather.23.cloned.1.call-done, bf16[8,12288]{1,0:T(8,128)(2,1)S(1)} %convert_reduce_fusion, f32[8]{0:T(128)S(1)} %convert_reduce_fusion.1), kind=kOutput, calls=%fused_computation.64 | convolution fusion | flops 201334784 | bytes 25395232 | tf_op jit(solution)/shard_map/dot_general | solution.py:78
  (115 shorter events, 84.1 us)
Async XLA Ops:
  7.2 466.5 %copy-start = (bf16[1536,1024]{1,0:T(8,128)(2,1)S(1)}, bf16[1536,1024]{1,0:T(8,128)(2,1)}, u32[]{:S(2)}) copy-start(bf16[1536,1024]{1,0:T(8,128)(2,1)} %param.13) | copy-start | bytes 9437188
  7.2 28.6 %all-gather.9.cloned.1.call-start = ((), (), s32[]{:S(2)}) async-start(), calls=%async_computation.6 | async-start | bytes 1474560 | tf_op jit(solution)/shard_map/all_gather | solution.py:35
  7.9 72.2 %reduce-scatter.19.cloned.1.call-start = ((), (), s32[]{:S(2)}) async-start(), calls=%async_computation.14 | async-start | bytes 1474560
  36.6 13.3 %collective-permute-start = (bf16[2,1536]{1,0:T(2,128)(2,1)S(1)}, bf16[2,1536]{1,0:T(2,128)(2,1)S(1)}, u32[]{:S(2)}, u32[]{:S(2)}) collective-permute-start(bf16[2,1536]{1,0:T(2,128)(2,1)S(1)} %get-tuple-element.18), channel_id=1, source_target_pairs={{0,4},{4,8},{8,12},{12,16},{16,20},{20,24},{24,28},{28,32},{32,36}... | collective-permute-start | bytes 18440 | tf_op jit(solution)/shard_map/ppermute | solution.py:18
  42.6 4.9 collective-permute-start.1
  56.2 25.8 %copy-start.6 = (bf16[384,384]{1,0:T(8,128)(2,1)S(1)}, bf16[384,384]{1,0:T(8,128)(2,1)}, u32[]{:S(2)}) copy-start(bf16[384,384]{1,0:T(8,128)(2,1)} %param.8) | copy-start | bytes 884740
  56.2 51.8 %all-gather.11.cloned.1.call-start = ((), (), s32[]{:S(2)}) async-start(), calls=%async_computation.7 | async-start | bytes 1474560 | tf_op jit(solution)/shard_map/all_gather | solution.py:35
  83.8 68.3 %reduce-scatter.21.cloned.1.call-start = ((), (), s32[]{:S(2)}) async-start(), calls=%async_computation.15 | async-start | bytes 1474560
  108.9 13.4 %collective-permute-start.2 = (bf16[4,1536]{1,0:T(4,128)(2,1)S(1)}, bf16[4,1536]{1,0:T(4,128)(2,1)S(1)}, u32[]{:S(2)}, u32[]{:S(2)}) collective-permute-start(bf16[4,1536]{1,0:T(4,128)(2,1)S(1)} %get-tuple-element.16), channel_id=1, source_target_pairs={{0,4},{4,8},{8,12},{12,16},{16,20},{20,24},{24,28},{28,32},{32,36}... | collective-permute-start | bytes 36872 | tf_op jit(solution)/shard_map/ppermute | solution.py:18
  114.9 5.0 collective-permute-start.3
  128.6 51.8 %all-gather.13.cloned.1.call-start = ((), (), s32[]{:S(2)}) async-start(), calls=%async_computation.8 | async-start | bytes 1474560 | tf_op jit(solution)/shard_map/all_gather | solution.py:35
  155.7 69.2 %reduce-scatter.23.cloned.1.call-start = ((), (), s32[]{:S(2)}) async-start(), calls=%async_computation.16 | async-start | bytes 1474560
  181.2 13.5 %collective-permute-start.4 = (bf16[8,1536]{1,0:T(8,128)(2,1)S(1)}, bf16[8,1536]{1,0:T(8,128)(2,1)S(1)}, u32[]{:S(2)}, u32[]{:S(2)}) collective-permute-start(bf16[8,1536]{1,0:T(8,128)(2,1)S(1)} %get-tuple-element.14), channel_id=1, source_target_pairs={{0,4},{4,8},{8,12},{12,16},{16,20},{20,24},{24,28},{28,32},{32,36}... | collective-permute-start | bytes 73736 | tf_op jit(solution)/shard_map/ppermute | solution.py:18
  187.2 5.1 collective-permute-start.5
  201.1 25.7 %copy-start.2 = (bf16[384,384]{1,0:T(8,128)(2,1)S(1)}, bf16[384,384]{1,0:T(8,128)(2,1)}, u32[]{:S(2)}) copy-start(bf16[384,384]{1,0:T(8,128)(2,1)} %add_convert_fusion.4) | copy-start | bytes 884740
  201.1 51.7 %all-gather.15.cloned.1.call-start = ((), (), s32[]{:S(2)}) async-start(), calls=%async_computation.9 | async-start | bytes 1474560 | tf_op jit(solution)/shard_map/all_gather | solution.py:35
  228.6 69.1 %reduce-scatter.25.cloned.1.call-start = ((), (), s32[]{:S(2)}) async-start(), calls=%async_computation.17 | async-start | bytes 1474560
  253.7 13.7 %collective-permute-start.6 = (bf16[16,1536]{1,0:T(8,128)(2,1)S(1)}, bf16[16,1536]{1,0:T(8,128)(2,1)S(1)}, u32[]{:S(2)}, u32[]{:S(2)}) collective-permute-start(bf16[16,1536]{1,0:T(8,128)(2,1)S(1)} %get-tuple-element.12), channel_id=1, source_target_pairs={{0,4},{4,8},{8,12},{12,16},{16,20},{20,24},{24,28},{28,32},{32,36}... | collective-permute-start | bytes 147464 | tf_op jit(solution)/shard_map/ppermute | solution.py:18
  259.7 5.4 collective-permute-start.7
  273.8 25.7 %copy-start.3 = (bf16[384,384]{1,0:T(8,128)(2,1)S(1)}, bf16[384,384]{1,0:T(8,128)(2,1)}, u32[]{:S(2)}) copy-start(bf16[384,384]{1,0:T(8,128)(2,1)} %add_convert_fusion.3) | copy-start | bytes 884740
  273.8 51.7 %all-gather.17.cloned.1.call-start = ((), (), s32[]{:S(2)}) async-start(), calls=%async_computation.10 | async-start | bytes 1474560 | tf_op jit(solution)/shard_map/all_gather | solution.py:35
  301.3 69.6 %reduce-scatter.27.cloned.1.call-start = ((), (), s32[]{:S(2)}) async-start(), calls=%async_computation.18 | async-start | bytes 1474560
  326.5 14.4 %collective-permute-start.8 = (bf16[32,1536]{1,0:T(8,128)(2,1)S(1)}, bf16[32,1536]{1,0:T(8,128)(2,1)S(1)}, u32[]{:S(2)}, u32[]{:S(2)}) collective-permute-start(bf16[32,1536]{1,0:T(8,128)(2,1)S(1)} %get-tuple-element.10), channel_id=1, source_target_pairs={{0,4},{4,8},{8,12},{12,16},{16,20},{20,24},{24,28},{28,32},{32,36}... | collective-permute-start | bytes 294920 | tf_op jit(solution)/shard_map/ppermute | solution.py:18
  332.7 5.9 %collective-permute-start.9 = (bf16[32,1536]{1,0:T(8,128)(2,1)S(1)}, bf16[32,1536]{1,0:T(8,128)(2,1)S(1)}, u32[]{:S(2)}, u32[]{:S(2)}) collective-permute-start(bf16[32,1536]{1,0:T(8,128)(2,1)S(1)} %get-tuple-element.11), channel_id=1, source_target_pairs={{4,0},{8,4},{12,8},{16,12},{20,16},{24,20},{28,24},{32,28},{36,32}... | collective-permute-start | bytes 294920 | tf_op jit(solution)/shard_map/ppermute | solution.py:20
  347.3 51.7 %all-gather.19.cloned.1.call-start = ((), (), s32[]{:S(2)}) async-start(), calls=%async_computation.11 | async-start | bytes 1474560 | tf_op jit(solution)/shard_map/all_gather | solution.py:35
  374.5 70.8 %reduce-scatter.29.cloned.1.call-start = ((), (), s32[]{:S(2)}) async-start(), calls=%async_computation.19 | async-start | bytes 1474560
  400.1 15.5 %collective-permute-start.10 = (bf16[64,1536]{1,0:T(8,128)(2,1)S(1)}, bf16[64,1536]{1,0:T(8,128)(2,1)S(1)}, u32[]{:S(2)}, u32[]{:S(2)}) collective-permute-start(bf16[64,1536]{1,0:T(8,128)(2,1)S(1)} %get-tuple-element.8), channel_id=1, source_target_pairs={{0,4},{4,8},{8,12},{12,16},{16,20},{20,24},{24,28},{28,32},{32,36}... | collective-permute-start | bytes 589832 | tf_op jit(solution)/shard_map/ppermute | solution.py:18
  406.2 7.0 %collective-permute-start.11 = (bf16[64,1536]{1,0:T(8,128)(2,1)S(1)}, bf16[64,1536]{1,0:T(8,128)(2,1)S(1)}, u32[]{:S(2)}, u32[]{:S(2)}) collective-permute-start(bf16[64,1536]{1,0:T(8,128)(2,1)S(1)} %get-tuple-element.9), channel_id=1, source_target_pairs={{4,0},{8,4},{12,8},{16,12},{20,16},{24,20},{28,24},{32,28},{36,32}... | collective-permute-start | bytes 589832 | tf_op jit(solution)/shard_map/ppermute | solution.py:20
  421.8 27.1 %copy-start.12 = (bf16[1024]{0:T(1024)(128)(2,1)S(1)}, bf16[1024]{0:T(1024)(128)(2,1)}, u32[]{:S(2)}) copy-start(bf16[1024]{0:T(1024)(128)(2,1)} %param.14) | copy-start | bytes 6148
  421.9 51.8 %all-gather.21.cloned.1.call-start = ((), (), s32[]{:S(2)}) async-start(), calls=%async_computation.12 | async-start | bytes 1474560 | tf_op jit(solution)/shard_map/all_gather | solution.py:71
  448.9 123.5 %all-gather.23.cloned.1.call-start = ((), (), s32[]{:S(2)}) async-start(), calls=%async_computation.13 | async-start | bytes 25952256 | tf_op jit(solution)/shard_map/all_gather | solution.py:76
  449.0 28.9 %copy-start.9 = (s32[8,64]{1,0:T(8,128)S(1)}, s32[8,64]{1,0:T(8,128)}, u32[]{:S(2)}) copy-start(s32[8,64]{1,0:T(8,128)} %param.15) | copy-start | bytes 6148
  (10 other events, 150.0 us)
Sparse Core Ops, SparseCore 0:
  9.7 26.0 all-gather.8
  56.3 23.7 reduce-scatter.18
  83.9 24.0 all-gather.10
  128.7 23.2 reduce-scatter.20
  155.8 24.5 all-gather.12
  201.2 23.6 reduce-scatter.22
  228.7 24.0 all-gather.14
  273.9 23.6 reduce-scatter.24
  301.4 24.1 all-gather.16
  347.4 23.4 reduce-scatter.26
  374.7 24.3 all-gather.18
  422.0 23.2 reduce-scatter.28
  449.1 24.5 all-gather.20
  478.0 94.4 all-gather.22
where the time goes:
time: 591 us; the launch traced here: 589 us
  waiting for transfers between devices  411 us (70%)
  matrix products  67.8 us (11%)
  starting transfers between devices  48.4 us (8%)
  local copies, waits for them, and re-layouts  31.5 us (5%)
  other arithmetic  16.6 us (3%)
  between operations  14.2 us (2%)
    all_gather x6, waiting for transfers between devices, dilated_inner(): gathered = lax.all_gather(trunk, 'trk', axis=1, tiled=True)  149 us
    unnamed x20, waiting for transfers between devices  142 us
    all_gather x1, waiting for transfers between devices, shards(): shard_rows = lax.all_gather(coverage, 'seq', axis=0, tiled=True)  89.5 us
    ppermute x6, starting transfers between devices, extended(): lax.ppermute(tail, axis, [(i, (i + 1) % count) for i in range(ends)])  36.1 us
    dot_general x12, matrix products, contract_last(): lax.dot_general(rows, kernel, (((1,), (1,)), ((), ())), preferred_element...  29.5 us
    unnamed x44, local copies, waits for them, and re-layouts  26 us
    all_gather x1, waiting for transfers between devices, shards(): lax.all_gather(trunk, 'trk', axis=1, tiled=True)  24.6 us
    dot_general x6, matrix products, shards(): jnp.dot(activation, conv_out[block_layer_index], preferred_element_type=j...  23.6 us
  transfers between devices with their start and end apart: 26, of which 20 were waited for; matrix products, arithmetic and copies ran while one was open for 6% of the time, Pallas kernels for 0%

commit v1 on v0

--- a/solution.py
+++ b/solution.py
@@ -73,7 +73,9 @@
         preferred_element_type=jnp.float32,
     )
     coverage = jax.nn.softplus(logits + head_bias.astype(jnp.float32)).astype(jnp.bfloat16)
-    shard_rows = lax.all_gather(coverage, "seq", axis=0, tiled=True)
+    shard_rows = jnp.concatenate(
+        lax.all_to_all(jnp.stack([coverage] * lax.axis_size("seq")), "seq", 0, 0), axis=0
+    )
     onehot = exon_onehot(exon_bins, shard_rows.shape[0])
     gene_sum = jnp.dot(onehot, shard_rows, preferred_element_type=jnp.float32)
     counts = jnp.sum((exon_bins >= 0).astype(jnp.float32), axis=1)

time: 591 us -> 912 us (1.54)
  the two profiles are of different devices: /device:TPU:1 before, /device:TPU:12 now
where the time goes in v1:
time: 912 us; the launch traced here: 910 us
  waiting for transfers between devices  736 us (81%)
  matrix products  67.1 us (7%)
  local copies, waits for them, and re-layouts  41 us (4%)
  starting transfers between devices  34.5 us (4%)
  other arithmetic  16.6 us (2%)
  between operations  14.2 us (2%)
    all_to_all x1, waiting for transfers between devices, shards(): lax.all_to_all(jnp.stack([coverage] * lax.axis_size('seq')), 'seq', 0, 0)  405 us
    unnamed x19, waiting for transfers between devices  153 us
    all_gather x6, waiting for transfers between devices, dilated_inner(): gathered = lax.all_gather(trunk, 'trk', axis=1, tiled=True)  153 us
    dot_general x12, matrix products, contract_last(): lax.dot_general(rows, kernel, (((1,), (1,)), ((), ())), preferred_element...  29.5 us
    unnamed x48, local copies, waits for them, and re-layouts  26.8 us
    all_gather x1, waiting for transfers between devices, shards(): lax.all_gather(trunk, 'trk', axis=1, tiled=True)  24.9 us
    dot_general x6, matrix products, shards(): jnp.dot(activation, conv_out[block_layer_index], preferred_element_type=j...  23.7 us
  transfers between devices with their start and end apart: 26, of which 14 were waited for; matrix products, arithmetic and copies ran while one was open for 4% of the time, Pallas kernels for 0%

profile of v1, /device:TPU:12, one launch (start us, length us, event | category | flops | bytes accessed | tf_op | source)
XLA Modules:
  0.0 909.8 jit_solution(13743148819214285229)
XLA Ops:
  8.9 28.2 %all-gather.8.cloned.1.call-done = bf16[384,1536]{1,0:T(8,128)(2,1)} async-done(((bf16[384,384]{1,0:T(8,128)(2,1)}), bf16[384,1536]{1,0:T(8,128)(2,1)}) %all-gather.8.cloned.1.call-update) | async-done | bytes 1179664 | tf_op jit(solution)/shard_map/all_gather | solution.py:35
  39.9 2.4 collective-permute-start
  46.7 3.9 convolution_convert_fusion.5
  53.7 24.9 %reduce-scatter.19.cloned.1.call-done = bf16[384,384]{1,0:T(8,128)(2,1)} async-done(((bf16[1536,384]{1,0:T(8,128)(2,1)}), bf16[384,384]{1,0:T(8,128)(2,1)}) %reduce-scatter.19.cloned.1.call-update) | async-done | bytes 294928
  82.3 24.9 %all-gather.10.cloned.1.call-done = bf16[384,1536]{1,0:T(8,128)(2,1)} async-done(((bf16[384,384]{1,0:T(8,128)(2,1)}), bf16[384,1536]{1,0:T(8,128)(2,1)}) %all-gather.10.cloned.1.call-update) | async-done | bytes 1179664 | tf_op jit(solution)/shard_map/all_gather | solution.py:35
  112.3 2.7 fusion.65
  117.4 4.0 convolution_convert_fusion.4
  123.8 25.5 %reduce-scatter.21.cloned.1.call-done = bf16[384,384]{1,0:T(8,128)(2,1)} async-done(((bf16[1536,384]{1,0:T(8,128)(2,1)}), bf16[384,384]{1,0:T(8,128)(2,1)}) %reduce-scatter.21.cloned.1.call-update) | async-done | bytes 294928
  153.1 24.9 %all-gather.12.cloned.1.call-done = bf16[384,1536]{1,0:T(8,128)(2,1)} async-done(((bf16[384,384]{1,0:T(8,128)(2,1)}), bf16[384,1536]{1,0:T(8,128)(2,1)}) %all-gather.12.cloned.1.call-update) | async-done | bytes 1179664 | tf_op jit(solution)/shard_map/all_gather | solution.py:35
  183.1 2.7 fusion.60
  188.1 4.0 convolution_convert_fusion.3
  194.6 25.6 %reduce-scatter.23.cloned.1.call-done = bf16[384,384]{1,0:T(8,128)(2,1)} async-done(((bf16[1536,384]{1,0:T(8,128)(2,1)}), bf16[384,384]{1,0:T(8,128)(2,1)}) %reduce-scatter.23.cloned.1.call-update) | async-done | bytes 294928
  223.8 24.8 %all-gather.14.cloned.1.call-done = bf16[384,1536]{1,0:T(8,128)(2,1)} async-done(((bf16[384,384]{1,0:T(8,128)(2,1)}), bf16[384,1536]{1,0:T(8,128)(2,1)}) %all-gather.14.cloned.1.call-update) | async-done | bytes 1179664 | tf_op jit(solution)/shard_map/all_gather | solution.py:35
  253.9 2.7 fusion.55
  258.9 4.0 convolution_convert_fusion.2
  265.4 25.5 %reduce-scatter.25.cloned.1.call-done = bf16[384,384]{1,0:T(8,128)(2,1)} async-done(((bf16[1536,384]{1,0:T(8,128)(2,1)}), bf16[384,384]{1,0:T(8,128)(2,1)}) %reduce-scatter.25.cloned.1.call-update) | async-done | bytes 294928
  294.6 24.9 %all-gather.16.cloned.1.call-done = bf16[384,1536]{1,0:T(8,128)(2,1)} async-done(((bf16[384,384]{1,0:T(8,128)(2,1)}), bf16[384,1536]{1,0:T(8,128)(2,1)}) %all-gather.16.cloned.1.call-update) | async-done | bytes 1179664 | tf_op jit(solution)/shard_map/all_gather | solution.py:35
  322.5 2.6 collective-permute-start.8
  325.1 2.7 fusion.50
  330.1 3.9 convolution_convert_fusion.1
  336.5 25.5 %reduce-scatter.27.cloned.1.call-done = bf16[384,384]{1,0:T(8,128)(2,1)} async-done(((bf16[1536,384]{1,0:T(8,128)(2,1)}), bf16[384,384]{1,0:T(8,128)(2,1)}) %reduce-scatter.27.cloned.1.call-update) | async-done | bytes 294928
  365.7 24.9 %all-gather.18.cloned.1.call-done = bf16[384,1536]{1,0:T(8,128)(2,1)} async-done(((bf16[384,384]{1,0:T(8,128)(2,1)}), bf16[384,1536]{1,0:T(8,128)(2,1)}) %all-gather.18.cloned.1.call-update) | async-done | bytes 1179664 | tf_op jit(solution)/shard_map/all_gather | solution.py:35
  396.1 2.7 fusion.45
  401.2 3.9 convolution_convert_fusion
  407.5 25.5 %reduce-scatter.29.cloned.1.call-done = bf16[384,384]{1,0:T(8,128)(2,1)} async-done(((bf16[1536,384]{1,0:T(8,128)(2,1)}), bf16[384,384]{1,0:T(8,128)(2,1)}) %reduce-scatter.29.cloned.1.call-update) | async-done | bytes 294928
  436.7 24.9 %all-gather.20.cloned.1.call-done = bf16[384,1536]{1,0:T(8,128)(2,1)} async-done(((bf16[384,384]{1,0:T(8,128)(2,1)}), bf16[384,1536]{1,0:T(8,128)(2,1)}) %all-gather.20.cloned.1.call-update) | async-done | bytes 1179664 | tf_op jit(solution)/shard_map/all_gather | solution.py:71
  461.6 3.3 fusion
  465.8 8.7 stack.2
  474.5 7.6 all-to-all-start
  482.2 4.9 convert_reduce_fusion
  487.2 405.4 %all-to-all-done = bf16[32,384,1024]{2,1,0:T(8,128)(2,1)} async-done(((bf16[32,384,1024]{2,1,0:T(8,128)(2,1)}), bf16[32,384,1024]{2,1,0:T(8,128)(2,1)}, u32[]{:S(2)}, u32[]{:S(2)}) %all-to-all-start) | async-done | bytes 25165856 | tf_op jit(solution)/shard_map/all_to_all | solution.py:77
  892.6 10.7 %convolution_divide_fusion = f32[8,1024]{1,0:T(8,128)} fusion(bf16[12288,1024]{1,0:T(8,128)(2,1)} %bitcast.30, bf16[8,12288]{1,0:T(8,128)(2,1)S(1)} %convert_reduce_fusion, f32[8]{0:T(128)S(1)} %convert_reduce_fusion.1), kind=kOutput, calls=%fused_computation.64 | convolution fusion | flops 201334784 | bytes 25395232 | tf_op jit(solution)/shard_map/dot_general | solution.py:80
  (119 shorter events, 82.9 us)
Async XLA Ops:
  7.2 454.4 %copy-start = (bf16[1536,1024]{1,0:T(8,128)(2,1)S(1)}, bf16[1536,1024]{1,0:T(8,128)(2,1)}, u32[]{:S(2)}) copy-start(bf16[1536,1024]{1,0:T(8,128)(2,1)} %param.13) | copy-start | bytes 9437188
  7.2 30.0 %all-gather.8.cloned.1.call-start = ((), (), s32[]{:S(2)}) async-start(), calls=%async_computation.7 | async-start | bytes 1474560 | tf_op jit(solution)/shard_map/all_gather | solution.py:35
  7.9 70.7 %reduce-scatter.19.cloned.1.call-start = ((), (), s32[]{:S(2)}) async-start(), calls=%async_computation.14 | async-start | bytes 1474560
  38.0 6.3 collective-permute-start.1
  39.9 6.8 collective-permute-start
  53.0 27.5 %copy-start.7 = (bf16[384,384]{1,0:T(8,128)(2,1)S(1)}, bf16[384,384]{1,0:T(8,128)(2,1)}, u32[]{:S(2)}) copy-start(bf16[384,384]{1,0:T(8,128)(2,1)} %param.8) | copy-start | bytes 884740
  53.0 54.2 %all-gather.10.cloned.1.call-start = ((), (), s32[]{:S(2)}) async-start(), calls=%async_computation.8 | async-start | bytes 1474560 | tf_op jit(solution)/shard_map/all_gather | solution.py:35
  82.2 67.2 %reduce-scatter.21.cloned.1.call-start = ((), (), s32[]{:S(2)}) async-start(), calls=%async_computation.15 | async-start | bytes 1474560
  108.0 7.0 collective-permute-start.3
  109.9 7.5 collective-permute-start.2
  123.8 27.5 %copy-start.6 = (bf16[384,384]{1,0:T(8,128)(2,1)S(1)}, bf16[384,384]{1,0:T(8,128)(2,1)}, u32[]{:S(2)}) copy-start(bf16[384,384]{1,0:T(8,128)(2,1)} %add_convert_fusion.5) | copy-start | bytes 884740
  123.8 54.1 %all-gather.12.cloned.1.call-start = ((), (), s32[]{:S(2)}) async-start(), calls=%async_computation.9 | async-start | bytes 1474560 | tf_op jit(solution)/shard_map/all_gather | solution.py:35
  153.0 67.1 %reduce-scatter.23.cloned.1.call-start = ((), (), s32[]{:S(2)}) async-start(), calls=%async_computation.16 | async-start | bytes 1474560
  178.8 7.0 collective-permute-start.5
  180.7 7.4 collective-permute-start.4
  194.5 27.5 %copy-start.3 = (bf16[384,384]{1,0:T(8,128)(2,1)S(1)}, bf16[384,384]{1,0:T(8,128)(2,1)}, u32[]{:S(2)}) copy-start(bf16[384,384]{1,0:T(8,128)(2,1)} %add_convert_fusion.4) | copy-start | bytes 884740
  194.5 54.1 %all-gather.14.cloned.1.call-start = ((), (), s32[]{:S(2)}) async-start(), calls=%async_computation.10 | async-start | bytes 1474560 | tf_op jit(solution)/shard_map/all_gather | solution.py:35
  223.8 67.1 %reduce-scatter.25.cloned.1.call-start = ((), (), s32[]{:S(2)}) async-start(), calls=%async_computation.17 | async-start | bytes 1474560
  249.6 7.0 collective-permute-start.7
  251.5 7.5 collective-permute-start.6
  265.3 27.5 %copy-start.4 = (bf16[384,384]{1,0:T(8,128)(2,1)S(1)}, bf16[384,384]{1,0:T(8,128)(2,1)}, u32[]{:S(2)}) copy-start(bf16[384,384]{1,0:T(8,128)(2,1)} %add_convert_fusion.3) | copy-start | bytes 884740
  265.3 54.1 %all-gather.16.cloned.1.call-start = ((), (), s32[]{:S(2)}) async-start(), calls=%async_computation.11 | async-start | bytes 1474560 | tf_op jit(solution)/shard_map/all_gather | solution.py:35
  294.5 67.5 %reduce-scatter.27.cloned.1.call-start = ((), (), s32[]{:S(2)}) async-start(), calls=%async_computation.18 | async-start | bytes 1474560
  320.4 7.3 collective-permute-start.9
  322.5 7.6 collective-permute-start.8
  336.5 54.1 %all-gather.18.cloned.1.call-start = ((), (), s32[]{:S(2)}) async-start(), calls=%async_computation.12 | async-start | bytes 1474560 | tf_op jit(solution)/shard_map/all_gather | solution.py:35
  365.7 67.4 %reduce-scatter.29.cloned.1.call-start = ((), (), s32[]{:S(2)}) async-start(), calls=%async_computation.19 | async-start | bytes 1474560
  391.6 7.2 collective-permute-start.11
  393.7 7.5 collective-permute-start.10
  407.5 29.2 %copy-start.14 = (bf16[1024]{0:T(1024)(128)(2,1)S(1)}, bf16[1024]{0:T(1024)(128)(2,1)}, u32[]{:S(2)}) copy-start(bf16[1024]{0:T(1024)(128)(2,1)} %param.14) | copy-start | bytes 6148
  407.5 54.1 %all-gather.20.cloned.1.call-start = ((), (), s32[]{:S(2)}) async-start(), calls=%async_computation.13 | async-start | bytes 1474560 | tf_op jit(solution)/shard_map/all_gather | solution.py:71
  474.5 418.1 %all-to-all-start = ((bf16[32,384,1024]{2,1,0:T(8,128)(2,1)}), bf16[32,384,1024]{2,1,0:T(8,128)(2,1)}, u32[]{:S(2)}, u32[]{:S(2)}) async-start(bf16[32,384,1024]{2,1,0:T(8,128)(2,1)} %stack.2), calls=%async_computation | async-start | bytes 50331648 | tf_op jit(solution)/shard_map/all_to_all | solution.py:77
  (12 other events, 120.2 us)
Sparse Core Ops, SparseCore 0:
  9.7 27.4 all-gather.7
  53.1 25.4 reduce-scatter.18
  82.3 24.7 all-gather.9
  123.9 25.4 reduce-scatter.20
  153.1 24.7 all-gather.11
  194.6 25.4 reduce-scatter.22
  223.9 24.7 all-gather.13
  265.4 25.4 reduce-scatter.24
  294.6 24.7 all-gather.15
  336.6 25.4 reduce-scatter.26
  365.8 24.7 all-gather.17
  407.6 25.4 reduce-scatter.28
  436.8 24.7 all-gather.19
